TPU v7x, 256 devices: a whole 4x4x8 slice. The times are simulated.
256 devices in a mesh: gr: 8 (over y, core), gc: 32 (over x, z).
Axes of the slice: x: 4, y: 4, z: 8, core: 2. Of those that a mesh axis runs over, the one named last changes fastest.
Arguments:
- below_factor: bfloat16 [31, 8, 64, 2, 32, 128], P(None, 'gr', None, None, 'gc'), may hold values from -0.046875 to 0.046875
- panel_factor: bfloat16 [31, 8, 64, 512], P(None, 'gr', 'gc'), may hold values from -0.046875 to 0.046875
- prior_factor: bfloat16 [512, 2, 32, 128], P('gr', None, 'gc'), may hold values from -0.25 to 0.25
- diag_factor: float32 [512, 512], replicated, may hold values from -1 to 3, as said below
- diag_inverse: float32 [512, 512], replicated, may hold values from -2 to 1, as said below
- below_adjoint: bfloat16 [31, 8, 64, 2, 32, 128], P(None, 'gr', None, None, 'gc'), may hold values from -6 to 6
- panel_adjoint: bfloat16 [31, 8, 64, 512], P(None, 'gr', 'gc'), may hold values from -6 to 6
- prior_adjoint: bfloat16 [512, 2, 32, 128], P('gr', None, 'gc'), may hold values from -6 to 6
- diag_adjoint: float32 [512, 512], replicated, may hold values from -6 to 6
Outputs:
- below_update: bfloat16 [31, 8, 64, 2, 32, 128], P(None, 'gr', None, None, 'gc')
- panel_gradient: bfloat16 [31, 8, 64, 512], P(None, 'gr', 'gc')
- prior_update: bfloat16 [512, 2, 32, 128], P('gr', None, 'gc')
- diag_gradient: float32 [512, 512], replicated
Inputs may be any that keep to these rules, and one draw needn't show every extreme that they name: `diag_factor`: lower triangular, diagonal entries positive. `diag_inverse`: the inverse of diag_factor.
All inputs are finite; a program needn't handle non-finite values.
Results may differ from a plain program's by a relative error of at most 0.015.
Values may be sent and summed in bfloat16 or wider, within the bound.
A program may use at most 64 MiB of HBM per device.

v0:
```python
import jax
import jax.numpy as jnp
from jax import lax
from jax.sharding import PartitionSpec as P


def row_product(left_rows, right_rows):
    return lax.dot_general(
        left_rows, right_rows, (((0,), (0,)), ((), ())), preferred_element_type=jnp.float32
    )


def diag_solve(diag_factor, diag_inverse, diag_reduced):
    highest = lax.Precision.HIGHEST
    chol_proj = jnp.dot(diag_factor.T, diag_reduced, precision=highest)
    phi_lower = jnp.tril(chol_proj) - 0.5 * jnp.diag(jnp.diagonal(chol_proj))
    symmetric = 0.5 * (phi_lower + phi_lower.T)
    left_side = jnp.dot(diag_inverse.T, symmetric, precision=highest)
    return jnp.dot(left_side, diag_inverse, precision=highest)


def local(
    below_factor,
    panel_factor,
    prior_factor,
    diag_factor,
    diag_inverse,
    below_adjoint,
    panel_adjoint,
    prior_adjoint,
    diag_adjoint,
):
    tile_count = below_factor.shape[0]
    tile_rows = below_factor.shape[2]
    local_rows = tile_count * tile_rows
    local_cols = below_factor.shape[3] * below_factor.shape[5]
    own_rows = panel_factor.shape[2]
    width = panel_factor.shape[3]
    prior_local = prior_factor.shape[0]
    below_mat = below_factor.reshape(local_rows, local_cols)
    below_bar = below_adjoint.reshape(local_rows, local_cols)
    inverse_bf = diag_inverse.astype(jnp.bfloat16)
    whole_bar, whole_factor = (
        lax.all_gather(panel_adjoint, "gc", axis=2, tiled=True),
        lax.all_gather(panel_factor, "gc", axis=2, tiled=True),
    )
    grad_rows = jnp.dot(
        whole_bar.reshape(local_rows, width), inverse_bf, preferred_element_type=jnp.float32
    ).astype(jnp.bfloat16)
    summed = lax.psum(
        row_product(grad_rows, whole_factor.reshape(local_rows, width)).astype(jnp.bfloat16), "gr"
    ).astype(jnp.float32)
    grid_col = lax.axis_index("gc")
    panel_grad = lax.dynamic_slice_in_dim(
        grad_rows.reshape(tile_count, 1, tile_rows, width), grid_col * own_rows, own_rows, 2
    )
    diag_reduced = jnp.tril(diag_adjoint - summed)
    diag_gradient = diag_solve(diag_factor, diag_inverse, diag_reduced)
    prior_here = prior_factor.reshape(prior_local, local_cols)
    prior_whole = lax.all_gather(prior_here, "gr", axis=0, tiled=True)
    below_new = (
        below_bar.astype(jnp.float32)
        - jnp.dot(grad_rows, prior_whole, preferred_element_type=jnp.float32)
    ).astype(jnp.bfloat16)
    crossing = lax.psum_scatter(
        row_product(grad_rows, below_mat).astype(jnp.bfloat16),
        "gr",
        scatter_dimension=0,
        tiled=True,
    ).astype(jnp.float32)
    grid_row = lax.axis_index("gr")
    twice_rows = lax.dynamic_slice_in_dim(
        2.0 * diag_gradient, grid_row * prior_local, prior_local, 0
    ).astype(jnp.bfloat16)
    curvature = jnp.dot(twice_rows, prior_whole, preferred_element_type=jnp.float32)
    prior_bar = prior_adjoint.reshape(prior_local, local_cols).astype(jnp.float32)
    prior_new = (prior_bar - crossing - curvature).astype(jnp.bfloat16)
    return (
        below_new.reshape(below_adjoint.shape),
        panel_grad,
        prior_new.reshape(prior_adjoint.shape),
        diag_gradient,
    )


def solution(mesh):
    in_specs = (
        P(None, "gr", None, None, "gc", None),
        P(None, "gr", "gc", None),
        P("gr", None, "gc", None),
        P(),
        P(),
        P(None, "gr", None, None, "gc", None),
        P(None, "gr", "gc", None),
        P("gr", None, "gc", None),
        P(),
    )
    out_specs = (
        P(None, "gr", None, None, "gc", None),
        P(None, "gr", "gc", None),
        P("gr", None, "gc", None),
        P(),
    )
    return jax.shard_map(local, mesh=mesh, in_specs=in_specs, out_specs=out_specs, check_vma=False)
```

profile of v0, /device:TPU:2, one launch (start us, length us, event | category | flops | bytes accessed | tf_op | source)
XLA Modules:
  0.0 281.4 jit_solution(9528895017282973600)
XLA Ops:
  7.2 0.0 copy-start
  7.2 0.0 all-gather.3.cloned.1.call-start
  7.2 1.6 copy.27
  8.8 0.0 all-gather.3.cloned.1.call-update
  8.8 0.0 all-gather.5.cloned.1.call-start
  8.9 1.5 copy.30
  10.3 0.0 all-gather.5.cloned.1.call-update
  10.4 0.0 all-reduce.2.cloned.1.call-start
  10.4 0.8 copy.46
  11.2 0.8 convert.3
  12.0 3.2 %convert.2 = f32[248,8,2,128]{3,2,1,0:T(2,128)} convert(bf16[248,8,2,128]{3,2,1,0:T(2,128)(2,1)} %bitcast.55) | non-fusion elementwise | flops 507904 | bytes 3047424
  15.2 13.3 %all_gather.10 = bf16[512,256]{1,0:T(8,128)(2,1)S(1)} all-gather(bf16[64,256]{1,0:T(8,128)(2,1)S(1)} %bitcast.57), channel_id=1, replica_groups=mesh['gr'=8,'gc'=32] {'gr'}, dimensions={0}, use_global_device_ids=true | all-gather | bytes 294912 | tf_op jit(solution)/shard_map/all_gather | solution.py:60
  28.5 62.4 %all-gather.3.cloned.1.call-done = bf16[31,1,64,512]{3,0,1,2:T(8,128)(2,1)} async-done(((bf16[31,1,2,512]{3,0,1,2:T(8,128)(2,1)}), bf16[31,1,64,512]{3,0,1,2:T(8,128)(2,1)}) %all-gather.3.cloned.1.call-update) | async-done | bytes 2031632 | tf_op jit(solution)/shard_map/all_gather | solution.py:44
  90.9 0.0 copy-start.2
  90.9 2.8 %copy.28 = bf16[31,1,64,512]{3,2,0,1:T(8,128)(2,1)S(1)} copy(bf16[31,1,64,512]{3,0,1,2:T(8,128)(2,1)} %all-gather.3.cloned.1.call-done) | data formatting | bytes 4063232 | tf_op jit(solution)/shard_map/all_gather | solution.py:44
  93.8 0.0 copy-done.2
  93.8 1.2 convolution_convert_fusion
  95.0 74.2 %all-gather.5.cloned.1.call-done = bf16[31,1,64,512]{3,0,1,2:T(8,128)(2,1)} async-done(((bf16[31,1,2,512]{3,0,1,2:T(8,128)(2,1)}), bf16[31,1,64,512]{3,0,1,2:T(8,128)(2,1)}) %all-gather.5.cloned.1.call-update) | async-done | bytes 2031632 | tf_op jit(solution)/shard_map/all_gather | solution.py:45
  169.2 2.7 copy.31
  172.0 2.1 convolution_convert_fusion.1
  174.1 0.0 all-reduce.2.cloned.1.call-update
  174.1 0.2 reduce-scatter.2.cloned.1.call-start
  174.3 3.2 %fusion = bf16[1984,256]{1,0:T(8,128)(2,1)} fusion(bf16[1984,512]{1,0:T(8,128)(2,1)S(1)} %convolution_convert_fusion, bf16[512,256]{1,0:T(8,128)(2,1)S(1)} %all_gather.10, f32[248,8,2,128]{3,2,1,0:T(2,128)} %convert.2), kind=kOutput, calls=%fused_computation.3 | convolution fusion | flops 521109504 | bytes 5341184 | tf_op jit(solution)/shard_map/dot_general | solution.py:63
  177.5 3.0 %reshape.38 = bf16[31,1,64,2,1,128]{5,3,2,0,4,1:T(2,128)(2,1)} reshape(bf16[1984,256]{1,0:T(8,128)(2,1)} %fusion) | data formatting | bytes 2031616 | tf_op jit(solution)/shard_map/reshape | solution.py:79
  180.6 0.7 constant_dynamic-slice_fusion
  181.3 2.7 convolution_convert_fusion.2
  184.0 0.0 reduce-scatter.2.cloned.1.call-update
  184.0 54.5 %all-reduce.2.cloned.1.call-done = bf16[512,512]{1,0:T(8,128)(2,1)} async-done(((bf16[512,512]{1,0:T(8,128)(2,1)}), bf16[512,512]{1,0:T(8,128)(2,1)}) %all-reduce.2.cloned.1.call-update) | async-done | bytes 524304 | tf_op jit(solution)/shard_map/psum | solution.py:50
  238.5 0.0 copy-done
  238.5 3.2 %fusion.13 = f32[512,512]{1,0:T(8,128)S(1)} fusion(f32[512,512]{1,0:T(8,128)S(1)} %copy-done, f32[512,512]{1,0:T(8,128)} %param.17, bf16[512,512]{1,0:T(8,128)(2,1)} %all-reduce.2.cloned.1.call-done), kind=kOutput, calls=%fused_computation.22 | convolution fusion | flops 1611661312 | bytes 3670016 | tf_op jit(solution)/shard_map/dot_general | solution.py:15
  241.7 0.3 copy.32
  242.1 4.5 %gather_fusion = f32[512]{0:T(512)S(1)} fusion(f32[512,512]{1,0:T(8,128)S(1)} %bitcast.51, s32[512]{0:T(512)S(1)} %bitcast.50), kind=kCustom, calls=%fused_computation | custom fusion | bytes 8192 | tf_op jit(solution)/shard_map/jit(diagonal)/cond/branch_0_fun/gather | solution.py:16
  246.6 0.0 copy-start.3
  246.6 3.4 %fusion.2 = f32[512,512]{1,0:T(8,128)S(1)} fusion(f32[512,512]{1,0:T(8,128)} %param.13, f32[512,512]{1,0:T(8,128)S(1)} %fusion.13, f32[512]{0:T(512)S(1)} %gather_fusion, f32[512,512]{0,1:T(8,128)S(1)} %copy.32), kind=kOutput, calls=%fused_computation.8 | convolution fusion | flops 1614282752 | bytes 4196352 | tf_op jit(solution)/shard_map/dot_general | solution.py:18
  250.0 0.0 copy-done.3
  250.0 1.9 fusion.34
  251.9 0.0 copy-start.1
  251.9 21.4 %reduce-scatter.2.cloned.1.call-done = bf16[64,256]{1,0:T(8,128)(2,1)} async-done(((bf16[512,256]{1,0:T(8,128)(2,1)}), bf16[64,256]{1,0:T(8,128)(2,1)}) %reduce-scatter.2.cloned.1.call-update) | async-done | bytes 32784 | tf_op jit(solution)/shard_map/reduce_scatter | solution.py:65
  273.3 0.9 fusion.1
  274.3 0.6 reshape.42
  274.9 0.0 copy-done.1
  (1 shorter events, 0.0 us)
Async XLA Ops:
  7.2 231.3 %copy-start = (f32[512,512]{1,0:T(8,128)S(1)}, f32[512,512]{1,0:T(8,128)}, u32[]{:S(2)}) copy-start(f32[512,512]{1,0:T(8,128)} %param.12) | copy-start | bytes 3145732
  7.2 83.7 %all-gather.3.cloned.1.call-start = ((), (), s32[]{:S(2)}) async-start(), calls=%async_computation.1 | async-start | bytes 2162688 | tf_op jit(solution)/shard_map/all_gather | solution.py:44
  8.8 160.4 %all-gather.5.cloned.1.call-start = ((), (), s32[]{:S(2)}) async-start(), calls=%async_computation.3 | async-start | bytes 2162688 | tf_op jit(solution)/shard_map/all_gather | solution.py:45
  10.4 228.1 %all-reduce.2.cloned.1.call-start = ((), (), s32[]{:S(2)}) async-start(), calls=%async_computation.4 | async-start | bytes 1048576 | tf_op jit(solution)/shard_map/psum | solution.py:50
  90.9 2.8 %copy-start.2 = (f32[512,512]{1,0:T(8,128)S(1)}, f32[512,512]{1,0:T(8,128)}, u32[]{:S(2)}) copy-start(f32[512,512]{1,0:T(8,128)} %param.13) | copy-start | bytes 3145732
  174.1 99.2 %reduce-scatter.2.cloned.1.call-start = ((), (), s32[]{:S(2)}) async-start(), calls=%async_computation.2 | async-start | bytes 294912 | tf_op jit(solution)/shard_map/reduce_scatter | solution.py:65
  246.6 3.4 %copy-start.3 = (f32[512,512]{1,0:T(8,128)S(1)}, f32[512,512]{1,0:T(8,128)}, u32[]{:S(2)}) copy-start(f32[512,512]{1,0:T(8,128)} %param.13) | copy-start | bytes 3145732
  251.9 23.0 %copy-start.1 = (f32[512,512]{1,0:T(8,128)}, f32[512,512]{1,0:T(8,128)S(1)}, u32[]{:S(2)}) copy-start(f32[512,512]{1,0:T(8,128)S(1)} %fusion.34) | copy-start | bytes 3145732
Sparse Core Ops, SparseCore 0:
  11.2 79.6 all-gather.2
  94.1 75.1 all-gather.4
  174.2 64.2 all-reduce.1
  241.0 32.2 reduce-scatter.1
where the time goes:
time: 282 us; the launch traced here: 281 us
  waiting for transfers between devices  213 us (76%)
  matrix products  18.7 us (7%)
  local copies, waits for them, and re-layouts  18.6 us (7%)
  between operations  13.9 us (5%)
  blocking collectives  13.3 us (5%)
  other arithmetic  3.99 us (1%)
    all_gather x1, waiting for transfers between devices, local(): lax.all_gather(panel_factor, 'gc', axis=2, tiled=True)  74.2 us
    all_gather x1, waiting for transfers between devices, local(): lax.all_gather(panel_adjoint, 'gc', axis=2, tiled=True)  62.4 us
    psum x1, waiting for transfers between devices, local(): lax.psum(row_product(grad_rows, whole_factor.reshape(local_rows, width))....  54.5 us
    reduce_scatter x1, waiting for transfers between devices, local(): lax.psum_scatter(row_product(grad_rows, below_mat).astype(jnp.bfloat16),...  21.4 us
    all_gather x1, blocking collectives, local(): prior_whole = lax.all_gather(prior_here, 'gr', axis=0, tiled=True)  13.3 us
  transfers between devices with their start and end apart: 4, of which 4 were waited for; matrix products, arithmetic and copies ran while one was open for 12% of the time, Pallas kernels for 0%

commit v1 on v0

--- a/solution.py
+++ b/solution.py
@@ -47,8 +47,12 @@
     grad_rows = jnp.dot(
         whole_bar.reshape(local_rows, width), inverse_bf, preferred_element_type=jnp.float32
     ).astype(jnp.bfloat16)
-    summed = lax.psum(
-        row_product(grad_rows, whole_factor.reshape(local_rows, width)).astype(jnp.bfloat16), "gr"
+    summed = jnp.sum(
+        lax.all_gather(
+            row_product(grad_rows, whole_factor.reshape(local_rows, width)).astype(jnp.bfloat16),
+            "gr",
+        ),
+        axis=0,
     ).astype(jnp.float32)
     grid_col = lax.axis_index("gc")
     panel_grad = lax.dynamic_slice_in_dim(

time: 282 us -> 251 us (0.89)
  waiting for transfers between devices: 213 us -> 178 us
    psum x1 -> x0, waiting for transfers between devices: 54.5 us -> none  [local(): lax.psum(row_product(grad_rows, whole_factor.reshape(local_rows, width))....]
    all_gather x1, waiting for transfers between devices: 62.4 us -> 80.5 us  [local(): lax.all_gather(panel_adjoint, 'gc', axis=2, tiled=True)]
    all_gather x0 -> x1, waiting for transfers between devices: none -> 6.93 us  [local(): lax.all_gather(row_product(grad_rows, whole_factor.reshape(local_rows, wi...]
    reduce_scatter x1, waiting for transfers between devices: 21.4 us -> 17.5 us  [local(): lax.psum_scatter(row_product(grad_rows, below_mat).astype(jnp.bfloat16),...]
    reduce_sum x0 -> x1, other arithmetic: none -> 3.14 us  [local(): jnp.sum(lax.all_gather(row_product(grad_rows, whole_factor.reshape(local_...]
  transfers between devices with their start and end apart: 4 -> 4, of which waited for: 4 -> 4; matrix products, arithmetic and copies ran while one was open for 12% -> 15% of each run, Pallas kernels for 0% -> 0%
where the time goes in v1:
time: 251 us
  waiting for transfers between devices  178 us (71%)
  matrix products  19.9 us (8%)
  local copies, waits for them, and re-layouts  19 us (8%)
  between operations  13.9 us (6%)
  blocking collectives  13.4 us (5%)
  other arithmetic  6.39 us (3%)
    all_gather x1, waiting for transfers between devices, local(): lax.all_gather(panel_adjoint, 'gc', axis=2, tiled=True)  80.5 us
    all_gather x1, waiting for transfers between devices, local(): lax.all_gather(panel_factor, 'gc', axis=2, tiled=True)  73.1 us
    reduce_scatter x1, waiting for transfers between devices, local(): lax.psum_scatter(row_product(grad_rows, below_mat).astype(jnp.bfloat16),...  17.5 us
    all_gather x1, blocking collectives, local(): prior_whole = lax.all_gather(prior_here, 'gr', axis=0, tiled=True)  13.4 us
    all_gather x1, waiting for transfers between devices, local(): lax.all_gather(row_product(grad_rows, whole_factor.reshape(local_rows, wi...  6.93 us
  transfers between devices with their start and end apart: 4, of which 4 were waited for; matrix products, arithmetic and copies ran while one was open for 15% of the time, Pallas kernels for 0%

profile of v1, /device:TPU:2, one launch (start us, length us, event | category | flops | bytes accessed | tf_op | source)
XLA Modules:
  0.0 250.9 jit_solution(7678820566448938203)
XLA Ops:
  7.2 0.0 copy-start
  7.2 0.0 all-gather.5.cloned.1.call-start
  7.2 1.6 copy.27
  8.8 0.0 all-gather.5.cloned.1.call-update
  8.8 0.0 all-gather.7.cloned.1.call-start
  8.9 1.5 copy.30
  10.3 0.0 all-gather.7.cloned.1.call-update
  10.4 0.0 all-gather.9.cloned.1.call-start
  10.4 80.5 %all-gather.5.cloned.1.call-done = bf16[31,1,64,512]{3,0,1,2:T(8,128)(2,1)} async-done(((bf16[31,1,2,512]{3,0,1,2:T(8,128)(2,1)}), bf16[31,1,64,512]{3,0,1,2:T(8,128)(2,1)}) %all-gather.5.cloned.1.call-update) | async-done | bytes 2031632 | tf_op jit(solution)/shard_map/all_gather | solution.py:44
  90.9 2.7 %copy.28 = bf16[31,1,64,512]{3,2,0,1:T(8,128)(2,1)S(1)} copy(bf16[31,1,64,512]{3,0,1,2:T(8,128)(2,1)} %all-gather.5.cloned.1.call-done) | data formatting | bytes 4063232 | tf_op jit(solution)/shard_map/all_gather | solution.py:44
  93.7 2.4 convolution_convert_fusion
  96.1 73.1 %all-gather.7.cloned.1.call-done = bf16[31,1,64,512]{3,0,1,2:T(8,128)(2,1)} async-done(((bf16[31,1,2,512]{3,0,1,2:T(8,128)(2,1)}), bf16[31,1,64,512]{3,0,1,2:T(8,128)(2,1)}) %all-gather.7.cloned.1.call-update) | async-done | bytes 2031632 | tf_op jit(solution)/shard_map/all_gather | solution.py:45
  169.2 2.7 %copy.31 = bf16[31,1,64,512]{3,2,0,1:T(8,128)(2,1)S(1)} copy(bf16[31,1,64,512]{3,0,1,2:T(8,128)(2,1)} %all-gather.7.cloned.1.call-done) | data formatting | bytes 4063232 | tf_op jit(solution)/shard_map/all_gather | solution.py:45
  172.0 0.0 copy-start.5
  172.0 0.0 copy-start.4
  172.0 2.1 convolution_convert_fusion.1
  174.1 0.0 all-gather.9.cloned.1.call-update
  174.1 0.0 reduce-scatter.2.cloned.1.call-start
  174.2 0.0 copy-done.5
  174.2 0.0 copy-done.4
  174.2 3.2 %convert.3 = f32[248,8,2,128]{3,2,1,0:T(2,128)} convert(bf16[248,8,2,128]{3,2,1,0:T(2,128)(2,1)} %bitcast.57) | non-fusion elementwise | flops 507904 | bytes 3047424
  177.5 13.4 %all_gather.16 = bf16[512,256]{1,0:T(8,128)(2,1)S(1)} all-gather(bf16[64,256]{1,0:T(8,128)(2,1)S(1)} %bitcast.59), channel_id=1, replica_groups=mesh['gr'=8,'gc'=32] {'gr'}, dimensions={0}, use_global_device_ids=true | all-gather | bytes 294912 | tf_op jit(solution)/shard_map/all_gather | solution.py:64
  190.8 3.3 %fusion = bf16[1984,256]{1,0:T(8,128)(2,1)} fusion(bf16[1984,512]{1,0:T(8,128)(2,1)S(1)} %convolution_convert_fusion, bf16[512,256]{1,0:T(8,128)(2,1)S(1)} %all_gather.16, f32[248,8,2,128]{3,2,1,0:T(2,128)} %convert.3), kind=kOutput, calls=%fused_computation.3 | convolution fusion | flops 521109504 | bytes 5341184 | tf_op jit(solution)/shard_map/dot_general | solution.py:67
  194.1 3.1 %reshape.38 = bf16[31,1,64,2,1,128]{5,3,2,0,4,1:T(2,128)(2,1)} reshape(bf16[1984,256]{1,0:T(8,128)(2,1)} %fusion) | data formatting | bytes 2031616 | tf_op jit(solution)/shard_map/reshape | solution.py:83
  197.2 2.7 %convolution_convert_fusion.2 = bf16[512,256]{1,0:T(8,128)(2,1)} fusion(bf16[1984,512]{1,0:T(8,128)(2,1)S(1)} %convolution_convert_fusion, bf16[248,8,2,128]{3,2,1,0:T(2,128)(2,1)} %bitcast.63), kind=kOutput, calls=%fused_computation.5 | convolution fusion | flops 520224768 | bytes 3309568 | tf_op jit(solution)/shard_map/dot_general | solution.py:8
  199.8 0.0 reduce-scatter.2.cloned.1.call-update
  199.9 0.7 constant_dynamic-slice_fusion
  200.6 6.9 %all-gather.9.cloned.1.call-done = bf16[4096,512]{1,0:T(8,128)(2,1)} async-done(((bf16[512,512]{1,0:T(8,128)(2,1)}), bf16[4096,512]{1,0:T(8,128)(2,1)}) %all-gather.9.cloned.1.call-update) | async-done | bytes 4194320 | tf_op jit(solution)/shard_map/all_gather | solution.py:51
  207.5 0.0 copy-start.2
  207.5 3.1 %reduce_sum.12 = bf16[512,512]{1,0:T(8,128)(2,1)S(1)} reduce(bf16[8,512,512]{2,1,0:T(8,128)(2,1)} %bitcast.55, bf16[]{:T(256)} %constant.28.clone.1), dimensions={0}, to_apply=%region_1.2 | reduce | flops 1835008 | bytes 4718594 | tf_op jit(solution)/shard_map/reduce_sum | solution.py:50
  210.7 0.0 copy-done
  210.7 0.0 copy-done.2
  210.7 2.9 %fusion.13 = f32[512,512]{1,0:T(8,128)} fusion(f32[512,512]{1,0:T(8,128)S(1)} %copy-done, f32[512,512]{1,0:T(8,128)S(1)} %copy-done.2, bf16[512,512]{1,0:T(8,128)(2,1)S(1)} %reduce_sum.12), kind=kOutput, calls=%fused_computation.22 | convolution fusion | flops 1611661312 | bytes 3670016 | tf_op jit(solution)/shard_map/dot_general | solution.py:15
  213.5 1.6 copy.32
  215.1 4.5 %gather_fusion = f32[512]{0:T(512)S(1)} fusion(f32[512,512]{1,0:T(8,128)S(1)} %bitcast.52, s32[512]{0:T(512)S(1)} %bitcast.51), kind=kCustom, calls=%fused_computation | custom fusion | bytes 8192 | tf_op jit(solution)/shard_map/jit(diagonal)/cond/branch_0_fun/gather | solution.py:16
  219.6 0.0 copy-start.3
  219.6 3.7 %fusion.2 = f32[512,512]{1,0:T(8,128)S(1)} fusion(f32[512,512]{1,0:T(8,128)} %param.13, f32[512,512]{1,0:T(8,128)} %fusion.13, f32[512]{0:T(512)S(1)} %gather_fusion, f32[512,512]{0,1:T(8,128)S(1)} %copy.32), kind=kOutput, calls=%fused_computation.8 | convolution fusion | flops 1614282752 | bytes 4196352 | tf_op jit(solution)/shard_map/dot_general | solution.py:18
  223.3 0.0 copy-done.3
  223.3 1.9 fusion.34
  225.2 0.0 copy-start.1
  225.3 17.5 %reduce-scatter.2.cloned.1.call-done = bf16[64,256]{1,0:T(8,128)(2,1)} async-done(((bf16[512,256]{1,0:T(8,128)(2,1)}), bf16[64,256]{1,0:T(8,128)(2,1)}) %reduce-scatter.2.cloned.1.call-update) | async-done | bytes 32784 | tf_op jit(solution)/shard_map/reduce_scatter | solution.py:69
  242.8 0.9 fusion.1
  243.7 0.6 reshape.42
  244.3 0.0 copy-done.1
  (3 shorter events, 0.0 us)
Async XLA Ops:
  7.2 203.5 %copy-start = (f32[512,512]{1,0:T(8,128)S(1)}, f32[512,512]{1,0:T(8,128)}, u32[]{:S(2)}) copy-start(f32[512,512]{1,0:T(8,128)} %param.12) | copy-start | bytes 3145732
  7.2 83.7 %all-gather.5.cloned.1.call-start = ((), (), s32[]{:S(2)}) async-start(), calls=%async_computation.1 | async-start | bytes 2162688 | tf_op jit(solution)/shard_map/all_gather | solution.py:44
  8.8 160.4 %all-gather.7.cloned.1.call-start = ((), (), s32[]{:S(2)}) async-start(), calls=%async_computation.3 | async-start | bytes 2162688 | tf_op jit(solution)/shard_map/all_gather | solution.py:45
  10.4 197.1 %all-gather.9.cloned.1.call-start = ((), (), s32[]{:S(2)}) async-start(), calls=%async_computation.4 | async-start | bytes 4718592 | tf_op jit(solution)/shard_map/all_gather | solution.py:51
  172.0 2.2 copy-start.5
  172.0 2.2 copy-start.4
  174.1 68.6 %reduce-scatter.2.cloned.1.call-start = ((), (), s32[]{:S(2)}) async-start(), calls=%async_computation.2 | async-start | bytes 294912 | tf_op jit(solution)/shard_map/reduce_scatter | solution.py:69
  207.5 3.2 %copy-start.2 = (f32[512,512]{1,0:T(8,128)S(1)}, f32[512,512]{1,0:T(8,128)}, u32[]{:S(2)}) copy-start(f32[512,512]{1,0:T(8,128)} %param.17) | copy-start | bytes 3145732
  219.6 3.7 %copy-start.3 = (f32[512,512]{1,0:T(8,128)S(1)}, f32[512,512]{1,0:T(8,128)}, u32[]{:S(2)}) copy-start(f32[512,512]{1,0:T(8,128)} %param.13) | copy-start | bytes 3145732
  225.2 19.1 %copy-start.1 = (f32[512,512]{1,0:T(8,128)}, f32[512,512]{1,0:T(8,128)S(1)}, u32[]{:S(2)}) copy-start(f32[512,512]{1,0:T(8,128)S(1)} %fusion.34) | copy-start | bytes 3145732
Sparse Core Ops, SparseCore 0:
  11.2 79.6 all-gather.4
  94.1 75.1 all-gather.6
  174.2 33.2 all-gather.8
  209.9 32.8 reduce-scatter.1
